TPU v7x, 32 devices: a whole 2x2x4 slice. The times are simulated.
32 devices in a mesh: row: 8 (over z, x), col: 4 (over y, core).
Axes of the slice: x: 2, y: 2, z: 4, core: 2. Of those that a mesh axis runs over, the one named last changes fastest.
Arguments:
- right_side: float32 [6, 8, 64, 128], P(None, 'row'), may hold values from -6 to 6
- inverses: float32 [6, 8, 128, 128], P(None, 'row'), may hold values from -1 to 3
- factor_blocks: bfloat16 [15, 8, 8, 128, 128], P(None, 'row', 'col'), may hold values from -0.15625 to 0.15625
- pattern: int32 [15, 8, 8], P(None, 'row', 'col'), may hold values 0 or 1
Outputs:
- forward_part: float32 [6, 8, 64, 128], P(None, 'row')
- solution: float32 [6, 8, 64, 128], P(None, 'row')
All inputs are finite; a program needn't handle non-finite values. No bound on the sum of `pattern` on one device may be relied on, other than what follows from the above.
Results may differ from a plain program's by a relative error of at most 0.014.
Values may be sent and summed in bfloat16 or wider, within the bound.
No kernel may reach another device: no remote copies, remote signals or barrier semaphores. Data moves between devices by JAX's collectives and lax.ppermute only.
A program may use at most 64 MiB of HBM per device.

v0:
```python
import jax
import jax.numpy as jnp
from jax import lax
from jax.sharding import PartitionSpec as P


def spread(block, axis, holder):
    block = jnp.where(lax.axis_index(axis) == holder, block, jnp.zeros_like(block))
    return lax.psum(block, axis)


def pair_number(higher, lower_level):
    return higher * (higher - 1) // 2 + lower_level


def masked_block(factor_blocks, pattern, pair_index):
    return jnp.where(
        pattern[pair_index][:, :, None, None] != 0,
        factor_blocks[pair_index],
        jnp.zeros((), factor_blocks.dtype),
    )


def shards(right_side, inverses, factor_blocks, pattern):
    levels = right_side.shape[0]
    width_col = factor_blocks.shape[2]
    row_index = lax.axis_index("row")
    col_index = lax.axis_index("col")
    solved = []
    gathered = []
    for height in range(levels):
        remaining = right_side[height]
        if height > 0:
            partial_value = jnp.zeros(remaining.shape, jnp.float32)
            for earlier in range(height):
                masked = masked_block(factor_blocks, pattern, pair_number(height, earlier))
                partial_value = partial_value + jnp.einsum(
                    "ikab,knb->ina", masked, gathered[earlier], preferred_element_type=jnp.float32
                )
            summed = lax.psum(partial_value.astype(jnp.bfloat16), "col").astype(jnp.float32)
            remaining = remaining - summed
        segment = jnp.einsum(
            "inb,iab->ina", remaining, inverses[height], precision=lax.Precision.HIGHEST
        )
        solved.append(segment)
        if height < levels - 1:
            gathered_all = lax.all_gather(segment.astype(jnp.bfloat16), "row", axis=0, tiled=True)
            gathered.append(
                lax.dynamic_slice_in_dim(gathered_all, col_index * width_col, width_col, 0)
            )
    results = [None] * levels
    settled = [None] * levels
    for height in range(levels - 1, -1, -1):
        remaining = solved[height]
        if height < levels - 1:
            partial_value = jnp.zeros((width_col,) + remaining.shape[1:], jnp.float32)
            for later in range(height + 1, levels):
                masked = masked_block(factor_blocks, pattern, pair_number(later, height))
                partial_value = partial_value + jnp.einsum(
                    "ikab,ina->knb", masked, settled[later], preferred_element_type=jnp.float32
                )
            offset = jnp.clip(row_index - col_index * width_col, 0, width_col - 1)
            owner_col = row_index // width_col
            summed = lax.psum(partial_value, "row")
            own_sum = lax.dynamic_slice_in_dim(summed, offset, 1, 0)
            own_sum = spread(own_sum.astype(jnp.bfloat16), "col", owner_col).astype(own_sum.dtype)
            remaining = remaining - own_sum
        segment = jnp.einsum(
            "ina,iab->inb", remaining, inverses[height], precision=lax.Precision.HIGHEST
        )
        results[height] = segment
        settled[height] = segment.astype(jnp.bfloat16)
    return (jnp.stack(solved), jnp.stack(results))


def solution(mesh):
    placed = (
        P(None, "row", None, None),
        P(None, "row", None, None),
        P(None, "row", "col", None, None),
        P(None, "row", "col"),
    )
    return jax.shard_map(
        shards,
        mesh=mesh,
        in_specs=placed,
        out_specs=(P(None, "row", None, None), P(None, "row", None, None)),
        check_vma=False,
    )
```

profile of v0, /device:TPU:0, one launch (start us, length us, event | category | flops | bytes accessed | tf_op | source)
XLA Modules:
  0.0 446.8 jit_solution(956539431709333284)
XLA Ops:
  0.7 1.7 compare_reduce_fusion
  2.3 1.1 bitcast_dynamic-update-slice_fusion.10
  3.5 32.3 %all-gather = bf16[512,128]{1,0:T(8,128)(2,1)S(1)} all-gather(bf16[64,128]{1,0:T(8,128)(2,1)S(1)} %convert_element_type.125), channel_id=2, replica_groups=mesh['row'=8,'col'=4] {'row'}, dimensions={0}, use_global_device_ids=true | all-gather | bytes 147456 | tf_op jit(solution)/shard_map/all_gather | solution.py:47
  35.8 1.0 fusion.24
  36.8 10.1 %psum.105 = bf16[1,64,128]{2,1,0:T(8,128)(2,1)S(1)} all-reduce(bf16[1,64,128]{2,1,0:T(8,128)(2,1)S(1)} %fusion.24), channel_id=1, replica_groups=mesh['row'=8,'col'=4] {'col'}, use_global_device_ids=true, to_apply=%region_0.1 | all-reduce | flops 8192 | bytes 32768 | tf_op jit(solution)/shard_map/psum | solution.py:40
  47.0 1.1 bitcast_dynamic-update-slice_fusion.9
  48.1 1.0 convolution_bitcast_fusion.15
  49.8 30.7 %all-gather.1 = bf16[512,128]{1,0:T(8,128)(2,1)S(1)} all-gather(bf16[64,128]{1,0:T(8,128)(2,1)S(1)} %convert_element_type.130), channel_id=3, replica_groups=mesh['row'=8,'col'=4] {'row'}, dimensions={0}, use_global_device_ids=true | all-gather | bytes 147456 | tf_op jit(solution)/shard_map/all_gather | solution.py:47
  80.7 10.1 %psum.106 = bf16[1,64,128]{2,1,0:T(8,128)(2,1)S(1)} all-reduce(bf16[1,64,128]{2,1,0:T(8,128)(2,1)S(1)} %fusion.23), channel_id=1, replica_groups=mesh['row'=8,'col'=4] {'col'}, use_global_device_ids=true, to_apply=%region_1.2 | all-reduce | flops 8192 | bytes 32768 | tf_op jit(solution)/shard_map/psum | solution.py:40
  91.3 0.2 fusion.8
  91.5 0.5 copy-done.2
  92.0 0.2 bitcast_dynamic-update-slice_fusion.8
  92.2 30.5 %all-gather.2 = bf16[512,128]{1,0:T(8,128)(2,1)S(1)} all-gather(bf16[64,128]{1,0:T(8,128)(2,1)S(1)} %convert_element_type.135), channel_id=4, replica_groups=mesh['row'=8,'col'=4] {'row'}, dimensions={0}, use_global_device_ids=true | all-gather | bytes 147456 | tf_op jit(solution)/shard_map/all_gather | solution.py:47
  123.0 10.1 %psum.107 = bf16[1,64,128]{2,1,0:T(8,128)(2,1)S(1)} all-reduce(bf16[1,64,128]{2,1,0:T(8,128)(2,1)S(1)} %fusion.22), channel_id=1, replica_groups=mesh['row'=8,'col'=4] {'col'}, use_global_device_ids=true, to_apply=%region_2.3 | all-reduce | flops 8192 | bytes 32768 | tf_op jit(solution)/shard_map/psum | solution.py:40
  133.5 0.3 bitcast_dynamic-update-slice_fusion.7
  133.8 30.5 %all-gather.3 = bf16[512,128]{1,0:T(8,128)(2,1)S(1)} all-gather(bf16[64,128]{1,0:T(8,128)(2,1)S(1)} %convert_element_type.140), channel_id=5, replica_groups=mesh['row'=8,'col'=4] {'row'}, dimensions={0}, use_global_device_ids=true | all-gather | bytes 147456 | tf_op jit(solution)/shard_map/all_gather | solution.py:47
  164.8 10.1 %psum.108 = bf16[1,64,128]{2,1,0:T(8,128)(2,1)S(1)} all-reduce(bf16[1,64,128]{2,1,0:T(8,128)(2,1)S(1)} %fusion.21), channel_id=1, replica_groups=mesh['row'=8,'col'=4] {'col'}, use_global_device_ids=true, to_apply=%region_3.4 | all-reduce | flops 8192 | bytes 32768 | tf_op jit(solution)/shard_map/psum | solution.py:40
  174.9 0.2 bitcast_dynamic-update-slice_fusion.6
  175.2 30.5 %all-gather.4 = bf16[512,128]{1,0:T(8,128)(2,1)S(1)} all-gather(bf16[64,128]{1,0:T(8,128)(2,1)S(1)} %convert_element_type.145), channel_id=6, replica_groups=mesh['row'=8,'col'=4] {'row'}, dimensions={0}, use_global_device_ids=true | all-gather | bytes 147456 | tf_op jit(solution)/shard_map/all_gather | solution.py:47
  205.9 10.1 %psum.109 = bf16[1,64,128]{2,1,0:T(8,128)(2,1)S(1)} all-reduce(bf16[1,64,128]{2,1,0:T(8,128)(2,1)S(1)} %fusion.20), channel_id=1, replica_groups=mesh['row'=8,'col'=4] {'col'}, use_global_device_ids=true, to_apply=%region_4.5 | all-reduce | flops 8192 | bytes 32768 | tf_op jit(solution)/shard_map/psum | solution.py:40
  216.0 0.2 bitcast_dynamic-update-slice_fusion.5
  216.7 37.5 %psum.110 = bf16[2,64,128]{2,1,0:T(8,128)(2,1)S(1)} all-reduce(f32[2,64,128]{2,1,0:T(8,128)S(1)} %convolution_bitcast_fusion), channel_id=1, replica_groups=mesh['row'=8,'col'=4] {'row'}, use_global_device_ids=true, to_apply=%region_5.6 | all-reduce | flops 16384 | bytes 98304 | tf_op jit(solution)/shard_map/psum | solution.py:64
  254.2 10.1 %psum.111 = bf16[1,64,128]{2,1,0:T(8,128)(2,1)S(1)} all-reduce(bf16[1,64,128]{2,1,0:T(8,128)(2,1)S(1)} %fusion.221), channel_id=1, replica_groups=mesh['row'=8,'col'=4] {'col'}, use_global_device_ids=true, to_apply=%region_6.7 | all-reduce | flops 8192 | bytes 32768 | tf_op jit(solution)/shard_map/psum | solution.py:9
  264.9 33.4 %psum.112 = bf16[2,64,128]{2,1,0:T(8,128)(2,1)S(1)} all-reduce(f32[2,64,128]{2,1,0:T(8,128)S(1)} %fusion.3), channel_id=1, replica_groups=mesh['row'=8,'col'=4] {'row'}, use_global_device_ids=true, to_apply=%region_7.8 | all-reduce | flops 16384 | bytes 98304 | tf_op jit(solution)/shard_map/psum | solution.py:64
  298.3 10.1 %psum.113 = bf16[1,64,128]{2,1,0:T(8,128)(2,1)S(1)} all-reduce(bf16[1,64,128]{2,1,0:T(8,128)(2,1)S(1)} %fusion.222), channel_id=1, replica_groups=mesh['row'=8,'col'=4] {'col'}, use_global_device_ids=true, to_apply=%region_8.9 | all-reduce | flops 8192 | bytes 32768 | tf_op jit(solution)/shard_map/psum | solution.py:9
  309.2 35.3 %psum.114 = bf16[2,64,128]{2,1,0:T(8,128)(2,1)S(1)} all-reduce(f32[2,64,128]{2,1,0:T(8,128)S(1)} %fusion.2), channel_id=1, replica_groups=mesh['row'=8,'col'=4] {'row'}, use_global_device_ids=true, to_apply=%region_9.10 | all-reduce | flops 16384 | bytes 98304 | tf_op jit(solution)/shard_map/psum | solution.py:64
  344.6 10.1 %psum.115 = bf16[1,64,128]{2,1,0:T(8,128)(2,1)S(1)} all-reduce(bf16[1,64,128]{2,1,0:T(8,128)(2,1)S(1)} %fusion.223), channel_id=1, replica_groups=mesh['row'=8,'col'=4] {'col'}, use_global_device_ids=true, to_apply=%region_10.11 | all-reduce | flops 8192 | bytes 32768 | tf_op jit(solution)/shard_map/psum | solution.py:9
  355.7 33.4 %psum.116 = bf16[2,64,128]{2,1,0:T(8,128)(2,1)S(1)} all-reduce(f32[2,64,128]{2,1,0:T(8,128)S(1)} %fusion.1), channel_id=1, replica_groups=mesh['row'=8,'col'=4] {'row'}, use_global_device_ids=true, to_apply=%region_11.12 | all-reduce | flops 16384 | bytes 98304 | tf_op jit(solution)/shard_map/psum | solution.py:64
  389.1 10.1 %psum.117 = bf16[1,64,128]{2,1,0:T(8,128)(2,1)S(1)} all-reduce(bf16[1,64,128]{2,1,0:T(8,128)(2,1)S(1)} %fusion.224), channel_id=1, replica_groups=mesh['row'=8,'col'=4] {'col'}, use_global_device_ids=true, to_apply=%region_12.13 | all-reduce | flops 8192 | bytes 32768 | tf_op jit(solution)/shard_map/psum | solution.py:9
  400.4 35.3 %psum.118 = bf16[2,64,128]{2,1,0:T(8,128)(2,1)S(1)} all-reduce(f32[2,64,128]{2,1,0:T(8,128)S(1)} %fusion), channel_id=1, replica_groups=mesh['row'=8,'col'=4] {'row'}, use_global_device_ids=true, to_apply=%region_13.14 | all-reduce | flops 16384 | bytes 98304 | tf_op jit(solution)/shard_map/psum | solution.py:64
  435.8 10.1 %psum.119 = bf16[1,64,128]{2,1,0:T(8,128)(2,1)S(1)} all-reduce(bf16[1,64,128]{2,1,0:T(8,128)(2,1)S(1)} %fusion.225), channel_id=1, replica_groups=mesh['row'=8,'col'=4] {'col'}, use_global_device_ids=true, to_apply=%region_14.15 | all-reduce | flops 8192 | bytes 32768 | tf_op jit(solution)/shard_map/psum | solution.py:9
  446.2 0.7 copy-done.4
  (56 shorter events, 6.8 us)
Async XLA Ops:
  0.6 48.5 %copy-start = (bf16[15,1,2,128,128]{4,3,2,1,0:T(8,128)(2,1)S(1)}, bf16[15,1,2,128,128]{4,3,2,1,0:T(8,128)(2,1)}, u32[]{:S(2)}) copy-start(bf16[15,1,2,128,128]{4,3,2,1,0:T(8,128)(2,1)} %param.6) | copy-start | bytes 2949124
  49.8 41.7 %copy-start.1 = (f32[6,1,128,128]{3,2,1,0:T(8,128)S(1)}, f32[6,1,128,128]{3,2,1,0:T(8,128)}, u32[]{:S(2)}) copy-start(f32[6,1,128,128]{3,2,1,0:T(8,128)} %param.5) | copy-start | bytes 1179652
  91.0 1.0 copy-start.2
  216.3 37.9 %copy-start.3 = (f32[6,1,64,128]{3,2,1,0:T(8,128)}, f32[6,1,64,128]{3,2,1,0:T(8,128)S(1)}, u32[]{:S(2)}) copy-start(f32[6,1,64,128]{3,2,1,0:T(8,128)S(1)} %get-tuple-element.27) | copy-start | bytes 589828
  446.1 0.7 copy-start.4
where the time goes:
time: 448 us; the launch traced here: 447 us
  blocking collectives  431 us (96%)
  matrix products  12.2 us (3%)
    psum x5, blocking collectives, shards(): summed = lax.psum(partial_value, 'row')  175 us
    all_gather x5, blocking collectives, shards(): lax.all_gather(segment.astype(jnp.bfloat16), 'row', axis=0, tiled=True)  155 us
    psum x5, blocking collectives, shards(): lax.psum(partial_value.astype(jnp.bfloat16), 'col').astype(jnp.float32)  50.7 us
    psum x5, blocking collectives, spread(): return lax.psum(block, axis)  50.6 us

commit v1 on v0

--- a/solution.py
+++ b/solution.py
@@ -2,6 +2,18 @@
 import jax.numpy as jnp
 from jax import lax
 from jax.sharding import PartitionSpec as P
+
+
+def _build_views(array_here, axis_name):
+    return jnp.concatenate(
+        lax.all_to_all(
+            jnp.stack([array_here for _ in range(lax.axis_size(axis_name))]),
+            axis_name=axis_name,
+            split_axis=0,
+            concat_axis=0,
+        ),
+        axis=0,
+    )
 
 
 def spread(block, axis, holder):
@@ -44,7 +56,7 @@
         )
         solved.append(segment)
         if height < levels - 1:
-            gathered_all = lax.all_gather(segment.astype(jnp.bfloat16), "row", axis=0, tiled=True)
+            gathered_all = _build_views(segment.astype(jnp.bfloat16), "row")
             gathered.append(
                 lax.dynamic_slice_in_dim(gathered_all, col_index * width_col, width_col, 0)
             )

time: 448 us -> 346 us (0.77)
  blocking collectives: 431 us -> 273 us
  waiting for transfers between devices: 0 us -> 32.6 us
  starting transfers between devices: 0 us -> 20.8 us
    all_gather x5 -> x0, blocking collectives: 155 us -> none  [shards(): lax.all_gather(segment.astype(jnp.bfloat16), 'row', axis=0, tiled=True)]
    all_to_all x0 -> x5, waiting for transfers between devices: none -> 32.6 us  [_build_views(): lax.all_to_all(jnp.stack([array_here for _ in range(lax.axis_size(axis_na...]
    all_to_all x0 -> x5, starting transfers between devices: none -> 20.8 us  [_build_views(): lax.all_to_all(jnp.stack([array_here for _ in range(lax.axis_size(axis_na...]
  transfers between devices with their start and end apart: 0 -> 5, of which waited for: 0 -> 5; matrix products, arithmetic and copies ran while one was open for 0% -> 1% of each run, Pallas kernels for 0% -> 0%
where the time goes in v1:
time: 346 us; the launch traced here: 345 us
  blocking collectives  273 us (79%)
  waiting for transfers between devices  32.6 us (9%)
  starting transfers between devices  20.8 us (6%)
  matrix products  11.3 us (3%)
  local copies, waits for them, and re-layouts  4.08 us (1%)
    psum x5, blocking collectives, shards(): summed = lax.psum(partial_value, 'row')  172 us
    psum x5, blocking collectives, shards(): lax.psum(partial_value.astype(jnp.bfloat16), 'col').astype(jnp.float32)  50.7 us
    psum x5, blocking collectives, spread(): return lax.psum(block, axis)  50.6 us
    all_to_all x5, waiting for transfers between devices, _build_views(): lax.all_to_all(jnp.stack([array_here for _ in range(lax.axis_size(axis_na...  32.6 us
    all_to_all x5, starting transfers between devices, _build_views(): lax.all_to_all(jnp.stack([array_here for _ in range(lax.axis_size(axis_na...  20.8 us
  transfers between devices with their start and end apart: 5, of which 5 were waited for; matrix products, arithmetic and copies ran while one was open for 1% of the time, Pallas kernels for 0%

profile of v1, /device:TPU:0, one launch (start us, length us, event | category | flops | bytes accessed | tf_op | source)
XLA Modules:
  0.0 344.9 jit_solution(7649832478856620124)
XLA Ops:
  0.7 1.2 bitcast_dynamic-update-slice_fusion.10
  1.9 0.7 stack.39
  2.5 7.3 %all-to-all-start = ((bf16[8,1,64,128]{3,2,1,0:T(8,128)(2,1)}), bf16[8,1,64,128]{3,2,1,0:T(8,128)(2,1)S(1)}, u32[]{:S(2)}, u32[]{:S(2)}) async-start(bf16[8,1,64,128]{3,2,1,0:T(8,128)(2,1)} %stack.39), calls=%async_computation | async-start | bytes 262144 | tf_op jit(solution)/shard_map/all_to_all | solution.py:9
  9.8 1.7 compare_reduce_fusion
  11.5 5.7 %all-to-all-done = bf16[8,1,64,128]{3,2,1,0:T(8,128)(2,1)S(1)} async-done(((bf16[8,1,64,128]{3,2,1,0:T(8,128)(2,1)}), bf16[8,1,64,128]{3,2,1,0:T(8,128)(2,1)S(1)}, u32[]{:S(2)}, u32[]{:S(2)}) %all-to-all-start) | async-done | bytes 131104 | tf_op jit(solution)/shard_map/all_to_all | solution.py:9
  17.2 1.0 fusion.24
  18.2 10.1 %psum.105 = bf16[1,64,128]{2,1,0:T(8,128)(2,1)S(1)} all-reduce(bf16[1,64,128]{2,1,0:T(8,128)(2,1)S(1)} %fusion.24), channel_id=1, replica_groups=mesh['row'=8,'col'=4] {'col'}, use_global_device_ids=true, to_apply=%region_0.1 | all-reduce | flops 8192 | bytes 32768 | tf_op jit(solution)/shard_map/psum | solution.py:52
  28.3 1.0 bitcast_dynamic-update-slice_fusion.9
  29.4 0.7 stack.41
  30.0 3.4 all-to-all-start.1
  34.3 6.4 %all-to-all-done.1 = bf16[8,1,64,128]{3,2,1,0:T(8,128)(2,1)S(1)} async-done(((bf16[8,1,64,128]{3,2,1,0:T(8,128)(2,1)}), bf16[8,1,64,128]{3,2,1,0:T(8,128)(2,1)S(1)}, u32[]{:S(2)}, u32[]{:S(2)}) %all-to-all-start.1) | async-done | bytes 131104 | tf_op jit(solution)/shard_map/all_to_all | solution.py:9
  40.9 10.1 %psum.106 = bf16[1,64,128]{2,1,0:T(8,128)(2,1)S(1)} all-reduce(bf16[1,64,128]{2,1,0:T(8,128)(2,1)S(1)} %fusion.23), channel_id=1, replica_groups=mesh['row'=8,'col'=4] {'col'}, use_global_device_ids=true, to_apply=%region_1.2 | all-reduce | flops 8192 | bytes 32768 | tf_op jit(solution)/shard_map/psum | solution.py:52
  51.3 0.7 stack.43
  52.0 3.4 all-to-all-start.2
  55.8 6.9 %all-to-all-done.2 = bf16[8,1,64,128]{3,2,1,0:T(8,128)(2,1)S(1)} async-done(((bf16[8,1,64,128]{3,2,1,0:T(8,128)(2,1)}), bf16[8,1,64,128]{3,2,1,0:T(8,128)(2,1)S(1)}, u32[]{:S(2)}, u32[]{:S(2)}) %all-to-all-start.2) | async-done | bytes 131104 | tf_op jit(solution)/shard_map/all_to_all | solution.py:9
  62.8 10.1 %psum.107 = bf16[1,64,128]{2,1,0:T(8,128)(2,1)S(1)} all-reduce(bf16[1,64,128]{2,1,0:T(8,128)(2,1)S(1)} %fusion.22), channel_id=1, replica_groups=mesh['row'=8,'col'=4] {'col'}, use_global_device_ids=true, to_apply=%region_2.3 | all-reduce | flops 8192 | bytes 32768 | tf_op jit(solution)/shard_map/psum | solution.py:52
  73.9 3.4 all-to-all-start.3
  77.7 6.9 %all-to-all-done.3 = bf16[8,1,64,128]{3,2,1,0:T(8,128)(2,1)S(1)} async-done(((bf16[8,1,64,128]{3,2,1,0:T(8,128)(2,1)}), bf16[8,1,64,128]{3,2,1,0:T(8,128)(2,1)S(1)}, u32[]{:S(2)}, u32[]{:S(2)}) %all-to-all-start.3) | async-done | bytes 131104 | tf_op jit(solution)/shard_map/all_to_all | solution.py:9
  84.8 10.1 %psum.108 = bf16[1,64,128]{2,1,0:T(8,128)(2,1)S(1)} all-reduce(bf16[1,64,128]{2,1,0:T(8,128)(2,1)S(1)} %fusion.21), channel_id=1, replica_groups=mesh['row'=8,'col'=4] {'col'}, use_global_device_ids=true, to_apply=%region_3.4 | all-reduce | flops 8192 | bytes 32768 | tf_op jit(solution)/shard_map/psum | solution.py:52
  95.8 3.4 all-to-all-start.4
  99.6 6.9 %all-to-all-done.4 = bf16[8,1,64,128]{3,2,1,0:T(8,128)(2,1)S(1)} async-done(((bf16[8,1,64,128]{3,2,1,0:T(8,128)(2,1)}), bf16[8,1,64,128]{3,2,1,0:T(8,128)(2,1)S(1)}, u32[]{:S(2)}, u32[]{:S(2)}) %all-to-all-start.4) | async-done | bytes 131104 | tf_op jit(solution)/shard_map/all_to_all | solution.py:9
  106.7 10.1 %psum.109 = bf16[1,64,128]{2,1,0:T(8,128)(2,1)S(1)} all-reduce(bf16[1,64,128]{2,1,0:T(8,128)(2,1)S(1)} %fusion.20), channel_id=1, replica_groups=mesh['row'=8,'col'=4] {'col'}, use_global_device_ids=true, to_apply=%region_4.5 | all-reduce | flops 8192 | bytes 32768 | tf_op jit(solution)/shard_map/psum | solution.py:52
  117.5 34.4 %psum.110 = bf16[2,64,128]{2,1,0:T(8,128)(2,1)S(1)} all-reduce(f32[2,64,128]{2,1,0:T(8,128)S(1)} %convolution_bitcast_fusion), channel_id=1, replica_groups=mesh['row'=8,'col'=4] {'row'}, use_global_device_ids=true, to_apply=%region_5.6 | all-reduce | flops 16384 | bytes 98304 | tf_op jit(solution)/shard_map/psum | solution.py:76
  152.0 10.1 %psum.111 = bf16[1,64,128]{2,1,0:T(8,128)(2,1)S(1)} all-reduce(bf16[1,64,128]{2,1,0:T(8,128)(2,1)S(1)} %fusion.236), channel_id=1, replica_groups=mesh['row'=8,'col'=4] {'col'}, use_global_device_ids=true, to_apply=%region_6.7 | all-reduce | flops 8192 | bytes 32768 | tf_op jit(solution)/shard_map/psum | solution.py:21
  162.7 34.4 %psum.112 = bf16[2,64,128]{2,1,0:T(8,128)(2,1)S(1)} all-reduce(f32[2,64,128]{2,1,0:T(8,128)S(1)} %fusion.3), channel_id=1, replica_groups=mesh['row'=8,'col'=4] {'row'}, use_global_device_ids=true, to_apply=%region_7.8 | all-reduce | flops 16384 | bytes 98304 | tf_op jit(solution)/shard_map/psum | solution.py:76
  197.1 10.1 %psum.113 = bf16[1,64,128]{2,1,0:T(8,128)(2,1)S(1)} all-reduce(bf16[1,64,128]{2,1,0:T(8,128)(2,1)S(1)} %fusion.237), channel_id=1, replica_groups=mesh['row'=8,'col'=4] {'col'}, use_global_device_ids=true, to_apply=%region_8.9 | all-reduce | flops 8192 | bytes 32768 | tf_op jit(solution)/shard_map/psum | solution.py:21
  208.0 34.4 %psum.114 = bf16[2,64,128]{2,1,0:T(8,128)(2,1)S(1)} all-reduce(f32[2,64,128]{2,1,0:T(8,128)S(1)} %fusion.2), channel_id=1, replica_groups=mesh['row'=8,'col'=4] {'row'}, use_global_device_ids=true, to_apply=%region_9.10 | all-reduce | flops 16384 | bytes 98304 | tf_op jit(solution)/shard_map/psum | solution.py:76
  242.5 10.1 %psum.115 = bf16[1,64,128]{2,1,0:T(8,128)(2,1)S(1)} all-reduce(bf16[1,64,128]{2,1,0:T(8,128)(2,1)S(1)} %fusion.238), channel_id=1, replica_groups=mesh['row'=8,'col'=4] {'col'}, use_global_device_ids=true, to_apply=%region_10.11 | all-reduce | flops 8192 | bytes 32768 | tf_op jit(solution)/shard_map/psum | solution.py:21
  253.6 34.4 %psum.116 = bf16[2,64,128]{2,1,0:T(8,128)(2,1)S(1)} all-reduce(f32[2,64,128]{2,1,0:T(8,128)S(1)} %fusion.1), channel_id=1, replica_groups=mesh['row'=8,'col'=4] {'row'}, use_global_device_ids=true, to_apply=%region_11.12 | all-reduce | flops 16384 | bytes 98304 | tf_op jit(solution)/shard_map/psum | solution.py:76
  288.0 10.1 %psum.117 = bf16[1,64,128]{2,1,0:T(8,128)(2,1)S(1)} all-reduce(bf16[1,64,128]{2,1,0:T(8,128)(2,1)S(1)} %fusion.239), channel_id=1, replica_groups=mesh['row'=8,'col'=4] {'col'}, use_global_device_ids=true, to_apply=%region_12.13 | all-reduce | flops 8192 | bytes 32768 | tf_op jit(solution)/shard_map/psum | solution.py:21
  299.4 34.4 %psum.118 = bf16[2,64,128]{2,1,0:T(8,128)(2,1)S(1)} all-reduce(f32[2,64,128]{2,1,0:T(8,128)S(1)} %fusion), channel_id=1, replica_groups=mesh['row'=8,'col'=4] {'row'}, use_global_device_ids=true, to_apply=%region_13.14 | all-reduce | flops 16384 | bytes 98304 | tf_op jit(solution)/shard_map/psum | solution.py:76
  333.8 10.1 %psum.119 = bf16[1,64,128]{2,1,0:T(8,128)(2,1)S(1)} all-reduce(bf16[1,64,128]{2,1,0:T(8,128)(2,1)S(1)} %fusion.240), channel_id=1, replica_groups=mesh['row'=8,'col'=4] {'col'}, use_global_device_ids=true, to_apply=%region_14.15 | all-reduce | flops 8192 | bytes 32768 | tf_op jit(solution)/shard_map/psum | solution.py:21
  (66 shorter events, 10.2 us)
Async XLA Ops:
  0.6 27.7 %copy-start.1 = (f32[6,1,128,128]{3,2,1,0:T(8,128)S(1)}, f32[6,1,128,128]{3,2,1,0:T(8,128)}, u32[]{:S(2)}) copy-start(f32[6,1,128,128]{3,2,1,0:T(8,128)} %param.5) | copy-start | bytes 1179652
  0.6 32.8 %copy-start = (bf16[15,1,2,128,128]{4,3,2,1,0:T(8,128)(2,1)S(1)}, bf16[15,1,2,128,128]{4,3,2,1,0:T(8,128)(2,1)}, u32[]{:S(2)}) copy-start(bf16[15,1,2,128,128]{4,3,2,1,0:T(8,128)(2,1)} %param.6) | copy-start | bytes 2949124
  2.5 14.6 %all-to-all-start = ((bf16[8,1,64,128]{3,2,1,0:T(8,128)(2,1)}), bf16[8,1,64,128]{3,2,1,0:T(8,128)(2,1)S(1)}, u32[]{:S(2)}, u32[]{:S(2)}) async-start(bf16[8,1,64,128]{3,2,1,0:T(8,128)(2,1)} %stack.39), calls=%async_computation | async-start | bytes 262144 | tf_op jit(solution)/shard_map/all_to_all | solution.py:9
  30.0 10.7 %all-to-all-start.1 = ((bf16[8,1,64,128]{3,2,1,0:T(8,128)(2,1)}), bf16[8,1,64,128]{3,2,1,0:T(8,128)(2,1)S(1)}, u32[]{:S(2)}, u32[]{:S(2)}) async-start(bf16[8,1,64,128]{3,2,1,0:T(8,128)(2,1)} %stack.41), calls=%async_computation.1 | async-start | bytes 262144 | tf_op jit(solution)/shard_map/all_to_all | solution.py:9
  34.1 17.0 %copy-start.2 = (f32[6,1,64,128]{3,2,1,0:T(8,128)S(1)}, f32[6,1,64,128]{3,2,1,0:T(8,128)}, u32[]{:S(2)}) copy-start(f32[6,1,64,128]{3,2,1,0:T(8,128)} %param.4) | copy-start | bytes 589828
  52.0 10.7 %all-to-all-start.2 = ((bf16[8,1,64,128]{3,2,1,0:T(8,128)(2,1)}), bf16[8,1,64,128]{3,2,1,0:T(8,128)(2,1)S(1)}, u32[]{:S(2)}, u32[]{:S(2)}) async-start(bf16[8,1,64,128]{3,2,1,0:T(8,128)(2,1)} %stack.43), calls=%async_computation.2 | async-start | bytes 262144 | tf_op jit(solution)/shard_map/all_to_all | solution.py:9
  73.9 10.7 %all-to-all-start.3 = ((bf16[8,1,64,128]{3,2,1,0:T(8,128)(2,1)}), bf16[8,1,64,128]{3,2,1,0:T(8,128)(2,1)S(1)}, u32[]{:S(2)}, u32[]{:S(2)}) async-start(bf16[8,1,64,128]{3,2,1,0:T(8,128)(2,1)} %stack.45), calls=%async_computation.3 | async-start | bytes 262144 | tf_op jit(solution)/shard_map/all_to_all | solution.py:9
  95.8 10.7 %all-to-all-start.4 = ((bf16[8,1,64,128]{3,2,1,0:T(8,128)(2,1)}), bf16[8,1,64,128]{3,2,1,0:T(8,128)(2,1)S(1)}, u32[]{:S(2)}, u32[]{:S(2)}) async-start(bf16[8,1,64,128]{3,2,1,0:T(8,128)(2,1)} %stack.47), calls=%async_computation.4 | async-start | bytes 262144 | tf_op jit(solution)/shard_map/all_to_all | solution.py:9
  117.1 34.9 %copy-start.3 = (f32[6,1,64,128]{3,2,1,0:T(8,128)}, f32[6,1,64,128]{3,2,1,0:T(8,128)S(1)}, u32[]{:S(2)}) copy-start(f32[6,1,64,128]{3,2,1,0:T(8,128)S(1)} %get-tuple-element.27) | copy-start | bytes 589828
  344.2 0.7 copy-start.4
